TPU v7x, 32 devices: a whole 2x2x4 slice. The times are simulated.
32 devices in a mesh: dom: 8 (over z, x), sub: 4 (over y, core).
Axes of the slice: x: 2, y: 2, z: 4, core: 2. Of those that a mesh axis runs over, the one named last changes fastest.
Arguments:
- unknowns: float32 [9, 56, 4096], P(None, None, ('dom', 'sub')), may hold values from -6 to 6
- jacobians: float32 [3, 9, 9, 4096], P(None, None, None, ('dom', 'sub')), may hold values from -2 to 2
- flux_local: float32 [4, 9, 9, 4096], P(None, None, None, ('dom', 'sub')), may hold values from -2 to 2
- flux_neighbour: float32 [4, 9, 9, 4096], P(None, None, None, ('dom', 'sub')), may hold values from -2 to 2
- stiffness: float32 [3, 56, 56], replicated, may hold values from -0.75 to 0.75
- volume_stiffness: float32 [3, 56, 56], replicated, may hold values from -0.375 to 0.375
- face_proj: float32 [4, 21, 56], replicated, may hold values from -0.75 to 0.75
- lift_back: float32 [4, 56, 21], replicated, may hold values from -0.625 to 0.625
- cluster: int32 [4096], P(('dom', 'sub')), may hold values from 0 to 2, as said below
- adjacent_column_index: int32 [4, 4096], P(None, ('dom', 'sub')), may hold values from 0 to 319, as said below
- neighbour_face: int32 [4, 4096], P(None, ('dom', 'sub')), may hold values from 0 to 3
- sub_sends: int32 [32, 4, 16], P(('dom', 'sub')), may hold values from 0 to 127
- dom_sends: int32 [32, 128], P(('dom', 'sub')), may hold values from 0 to 127
Outputs:
- updated: float32 [9, 56, 4096], P(None, None, ('dom', 'sub'))
Inputs may be any that keep to these rules, and one draw needn't show every extreme that they name: On every device the elements are ordered by cluster, never falling; at most 32 of a device's elements are in cluster 0 and at most 64 in clusters 0 and 1; some device has exactly 32 in cluster 0 and some exactly 64 in clusters 0 and 1. `adjacent_column_index`: values below 128 name elements of the same device; each of the 192 columns from 128 on is named by exactly one face of each device.
All inputs are finite; a program needn't handle non-finite values.
Results may differ from a plain program's by a relative error of at most 0.0001.
Values sent between devices are 32-bit elements; how exact they have to be, the bound alone decides.
A program may use at most 128 MiB of HBM per device.

v0:
```python
import functools
import math

import jax
import jax.numpy as jnp
from jax import lax
from jax.experimental import pallas as pl
from jax.experimental.pallas import tpu as pltpu
from jax.sharding import PartitionSpec as P

ORDER = 6
TICKS = 4
TICK_LENGTH = 0.25
F32 = jnp.float32
BF16 = jnp.bfloat16
MESH = pl.DeviceIdType.MESH


def taylor_weights(order_count):
    return [
        [
            TICK_LENGTH ** (k + 1) * ((a + 1) ** (k + 1) - a ** (k + 1)) / math.factorial(k + 1)
            for k in range(order_count)
        ]
        for a in range(TICKS)
    ]


def round_up(n, m):
    return -(-n // m) * m


def split(x):
    hi = x.astype(BF16).astype(F32)
    return hi, x - hi


def stacked_rhs(fields):
    blocks = []
    for v in fields:
        hi, lo = split(v)
        blocks.append(jnp.concatenate([hi, lo, hi], axis=0).astype(BF16))
    return jnp.concatenate(blocks, axis=1)


def dot(a, b):
    return jnp.dot(a, b, preferred_element_type=F32)


def kernel(
    sizes,
    u_ref, jac_ref, fl_ref, fn_ref, w_ref, lift_ref, len_ref, adj_ref, nf_ref, send_ref,
    out_ref,
    cur, piece, own, acc_g, proj, tproj, tr, oh, ohs, wl, jin, jrecv, outbuf, arr,
    ssem, rsem, jssem, jrsem,
):
    Q, B, E, FB, n_dom, n_sub, hs, hd = sizes
    R = n_sub * hs + 2 * hd
    RP = arr.shape[1]
    S = n_sub * hs
    nd, ns = 3 * B, 4 * FB
    i_dom, i_sub = lax.axis_index("dom"), lax.axis_index("sub")
    nxt, prv = lax.rem(i_dom + 1, n_dom), lax.rem(i_dom + n_dom - 1, n_dom)
    peers = [lax.rem(i_sub + o, n_sub) for o in range(1, n_sub)]

    barrier = pltpu.get_barrier_semaphore()
    targets = [(i_dom, p) for p in peers] + [(nxt, i_sub), (prv, i_sub)]
    for tgt in targets:
        pl.semaphore_signal(barrier, inc=1, device_id=tgt, device_id_type=MESH)
    pl.semaphore_wait(barrier, len(targets))

    def copies(src, dst, ss, rs):
        made = []
        for o in range(1, n_sub):
            p = peers[o - 1]
            made.append(pltpu.make_async_remote_copy(
                src_ref=src.at[pl.ds(pl.multiple_of(p * hs, 8), hs)],
                dst_ref=dst.at[pl.ds(pl.multiple_of(i_sub * hs, 8), hs)],
                send_sem=ss.at[o - 1], recv_sem=rs.at[o - 1],
                device_id=(i_dom, p), device_id_type=MESH))
        for o, (tgt, a, b) in enumerate([(nxt, S + hd, S), (prv, S, S + hd)]):
            made.append(pltpu.make_async_remote_copy(
                src_ref=src.at[pl.ds(a, hd)], dst_ref=dst.at[pl.ds(b, hd)],
                send_sem=ss.at[n_sub - 1 + o], recv_sem=rs.at[n_sub - 1 + o],
                device_id=(tgt, i_sub), device_id_type=MESH))
        return made

    def self_rows(src, dst):
        rows = pl.ds(pl.multiple_of(i_sub * hs, 8), hs)
        dst[rows, :] = src[rows, :]

    wanted = jnp.zeros((RP, 1), F32)
    for i in range(4):
        adj = adj_ref[pl.ds(i, 1), :]
        nf = nf_ref[pl.ds(i, 1), :]
        key = jnp.where(adj < E, nf * E + adj, -1)
        rows = lax.broadcasted_iota(jnp.int32, (4 * E, E), 0)
        oh[pl.ds(0, 4 * E), pl.ds(i * E, E)] = jnp.where(rows == key, 1.0, 0.0).astype(BF16)
        rows = lax.broadcasted_iota(jnp.int32, (RP, E), 0) + E
        hit = rows == adj
        oh[pl.ds(4 * E, RP), pl.ds(i * E, E)] = jnp.where(hit, 1.0, 0.0).astype(BF16)
        wanted = wanted + jnp.sum(
            jnp.where(hit, nf.astype(F32), 0.0), axis=1, keepdims=True)
    jin[...] = jnp.broadcast_to(wanted[:R], (R, 128))
    first = copies(jin, jrecv, jssem, jrsem)
    for c in first:
        c.start()
    self_rows(jin, jrecv)

    if RP > R:
        for t in range(TICKS):
            arr[t, pl.ds(R, RP - R), :] = jnp.zeros((RP - R, arr.shape[2]), F32)
    out_ref[...] = u_ref[...]
    own[...] = jnp.zeros_like(own)
    acc_g[...] = jnp.zeros_like(acc_g)

    def contract(dst):
        for q0 in range(0, Q, 3):
            sums = [None] * 3
            for d in range(3):
                for p in range(Q):
                    v = proj[pl.ds(d * B, B), pl.ds(p * E, E)]
                    for g in range(3):
                        term = jac_ref[d, p, pl.ds(q0 + g, 1), :] * v
                        sums[g] = term if sums[g] is None else sums[g] + term
            for g in range(3):
                dst(q0 + g, sums[g])

    def put_cur(q, v):
        cur[q] = v

    weights = taylor_weights(ORDER)
    length = len_ref[...]

    def flux(solver, i, trace):
        sums = [None] * Q
        for p in range(Q):
            v = trace(p)
            for q in range(Q):
                term = solver[i, p, pl.ds(q, 1), :] * v
                sums[q] = term if sums[q] is None else sums[q] + term
        return sums

    def tick(t, carry):
        phase = t & (length - 1)
        for k in range(ORDER):
            row = jnp.full((1, E), weights[0][k], F32)
            for a in range(1, TICKS):
                row = jnp.where(phase == a, F32(weights[a][k]), row)
            wl[pl.ds(k, 1), :] = row
        w0 = wl[pl.ds(0, 1), :]
        for p in range(Q):
            v = out_ref[p]
            cur[p] = v
            piece[p] = w0 * v

        def order_step(k, c):
            proj[...] = dot(w_ref[pl.ds(0, nd), :], stacked_rhs([cur[p] for p in range(Q)]))
            wk = wl[pl.ds(k, 1), :]

            def put(q, v):
                cur[q] = v
                piece[q] = piece[q] + wk * v

            contract(put)
            return c

        lax.fori_loop(1, ORDER, order_step, 0)

        tproj[...] = dot(
            w_ref[pl.ds(2 * nd, ns), :], stacked_rhs([piece[p] for p in range(Q)]))
        for p in range(Q):
            for j in range(4):
                tr[pl.ds(p * FB, FB), pl.ds(j * E, E)] = tproj[
                    pl.ds(j * FB, FB), pl.ds(p * E, E)]

        @pl.when(t == 0)
        def _():
            for c in first:
                c.wait()
            want = jrecv[...]
            for j in range(4):
                lane = lax.broadcasted_iota(jnp.int32, (R, E), 1)
                same = jnp.where(lane == send_ref[...], 1.0, 0.0)
                face = jnp.where(want == F32(j), 1.0, 0.0)
                ohs[:, pl.ds(j * E, E)] = (same * face).astype(BF16)

        hi, lo = split(tr[...])
        hi, lo = hi.astype(BF16), lo.astype(BF16)
        nt = (((1,), (1,)), ((), ()))
        o = ohs[...]
        outbuf[t] = (lax.dot_general(o, hi, nt, preferred_element_type=F32)
                     + lax.dot_general(o, lo, nt, preferred_element_type=F32))
        sent = copies(outbuf.at[t], arr.at[t], ssem.at[t], rsem.at[t])
        for c in sent:
            c.start()
        self_rows(outbuf.at[t], arr.at[t])

        for p in range(Q):
            own[p] = own[p] + piece[p]
        rhs = stacked_rhs([own[p] for p in range(Q)])
        proj[...] = dot(w_ref[pl.ds(nd, nd), :], rhs)
        tproj[...] = dot(w_ref[pl.ds(2 * nd, ns), :], rhs)
        contract(put_cur)
        ohl = oh[pl.ds(0, 4 * E), :]
        gathered = dot(hi, ohl) + dot(lo, ohl)

        for c in sent:
            c.wait()
        at = arr[t].T
        ahi, alo = split(at)
        oha = oh[pl.ds(4 * E, RP), :]
        gathered = gathered + dot(ahi.astype(BF16), oha) + dot(alo.astype(BF16), oha)
        tr[...] = gathered

        finished = ((t + 1) & (length - 1)) == 0
        for i in range(4):
            rows = pl.ds(i * FB, FB)
            there = flux(fn_ref, i, lambda p: tr[pl.ds(p * FB, FB), pl.ds(i * E, E)])
            for q in range(Q):
                acc_g[q, rows, :] = acc_g[q, rows, :] + there[q]
            here = flux(fl_ref, i, lambda p: tproj[rows, pl.ds(p * E, E)])
            for q in range(Q):
                proj[rows, pl.ds(q * E, E)] = acc_g[q, rows, :] + here[q]
        lifted = dot(
            lift_ref[...], stacked_rhs([proj[pl.ds(0, ns), pl.ds(q * E, E)] for q in range(Q)]))
        for q in range(Q):
            change = cur[q] - lifted[:, q * E:(q + 1) * E]
            out_ref[q] = jnp.where(finished, out_ref[q] + change, out_ref[q])
            own[q] = jnp.where(finished, 0.0, own[q])
            acc_g[q] = jnp.where(finished, 0.0, acc_g[q])
        return carry

    lax.fori_loop(0, TICKS, tick, 0)


def three_terms(m):
    hi = lax.reduce_precision(m, 8, 7)
    lo = lax.reduce_precision(m - hi, 8, 7)
    return jnp.concatenate([hi, hi, lo], axis=1).astype(BF16)


def local(
    n_dom, n_sub,
    unknowns, jacobians, flux_local, flux_neighbour, stiffness, volume_stiffness,
    face_proj, lift_back, cluster, adjacent_column_index, neighbour_face, sub_sends, dom_sends,
):
    Q, B, E = unknowns.shape
    fb = face_proj.shape[1]
    FB = round_up(fb, 8)
    hs = sub_sends.shape[2]
    hd = dom_sends.shape[1] // 2
    R = n_sub * hs + 2 * hd
    RP = round_up(R, 128)
    pad = ((0, 0), (0, FB - fb), (0, 0))
    w = three_terms(jnp.concatenate([
        stiffness.reshape(3 * B, B), volume_stiffness.reshape(3 * B, B),
        jnp.pad(face_proj, pad).reshape(4 * FB, B)], axis=0))
    lift = three_terms(
        jnp.pad(lift_back.transpose(1, 0, 2), pad[:1] + ((0, 0), (0, FB - fb))).reshape(B, 4 * FB))
    length = jnp.left_shift(1, cluster).astype(jnp.int32).reshape(1, E)
    sends = jnp.concatenate([sub_sends[0].reshape(-1), dom_sends[0]])
    sends = jnp.broadcast_to(sends[:, None], (R, E))
    sizes = (Q, B, E, FB, n_dom, n_sub, hs, hd)
    peers = n_sub + 1
    vm = pl.BlockSpec(memory_space=pltpu.VMEM)
    W = Q * FB
    return pl.pallas_call(
        functools.partial(kernel, sizes),
        out_shape=jax.ShapeDtypeStruct(unknowns.shape, F32),
        in_specs=[vm] * 10,
        out_specs=vm,
        scratch_shapes=[
            pltpu.VMEM((Q, B, E), F32),
            pltpu.VMEM((Q, B, E), F32),
            pltpu.VMEM((Q, B, E), F32),
            pltpu.VMEM((Q, 4 * FB, E), F32),
            pltpu.VMEM((3 * B, Q * E), F32),
            pltpu.VMEM((4 * FB, Q * E), F32),
            pltpu.VMEM((W, 4 * E), F32),
            pltpu.VMEM((4 * E + RP, 4 * E), BF16),
            pltpu.VMEM((R, 4 * E), BF16),
            pltpu.VMEM((8, E), F32),
            pltpu.VMEM((R, 128), F32),
            pltpu.VMEM((R, 128), F32),
            pltpu.VMEM((TICKS, R, W), F32),
            pltpu.VMEM((TICKS, RP, W), F32),
            pltpu.SemaphoreType.DMA((TICKS, peers)),
            pltpu.SemaphoreType.DMA((TICKS, peers)),
            pltpu.SemaphoreType.DMA((peers,)),
            pltpu.SemaphoreType.DMA((peers,)),
        ],
        compiler_params=pltpu.CompilerParams(collective_id=0, has_side_effects=True),
    )(unknowns, jacobians, flux_local, flux_neighbour, w, lift, length,
      adjacent_column_index, neighbour_face, sends)


def solution(mesh):
    both = ("dom", "sub")
    in_specs = (
        P(None, None, both), P(None, None, None, both), P(None, None, None, both),
        P(None, None, None, both), P(), P(), P(), P(), P(both), P(None, both), P(None, both),
        P(both, None, None), P(both, None),
    )
    fn = functools.partial(local, mesh.shape["dom"], mesh.shape["sub"])
    return jax.shard_map(
        fn, mesh=mesh, in_specs=in_specs, out_specs=P(None, None, both), check_vma=False)
```

profile of v0, /device:TPU:0, one launch (start us, length us, event | category | flops | bytes accessed | tf_op | source)
XLA Modules:
  0.0 60.5 jit_solution(14495672217338616560)
XLA Ops:
  0.0 0.7 %copy-done.8 = s32[128]{0:T(128)S(1)} copy-done((s32[128]{0:T(128)S(1)}, s32[128]{0:T(128)}, u32[]{:S(2)}) %copy-start.8) | copy-done | bytes 536
  0.7 0.5 shift-left_bitcast_fusion.len_ref
  1.1 0.0 copy-done.6
  1.1 0.1 reshape_squeeze.3
  1.2 0.6 copy-done.7
  1.8 0.1 pad_add_fusion
  1.9 0.8 %copy.26 = f32[4,21,56]{2,1,0:T(8,128)S(1)} copy(f32[4,21,56]{2,0,1:T(4,128)} %param.19) | data formatting | bytes 37632
  2.7 0.8 %copy-done.5 = f32[4,56,21]{1,0,2:T(4,128)S(1)} copy-done((f32[4,56,21]{1,0,2:T(4,128)S(1)}, f32[4,56,21]{1,0,2:T(4,128)}, u32[]{:S(2)}) %copy-start.5) | copy-done | bytes 18840
  3.5 0.1 copy.21
  3.6 0.0 copy-start.3
  3.6 0.0 copy-start.4
  3.6 0.7 %pad_maximum_fusion.2.lift_ref = bf16[56,288]{1,0:T(8,128)(2,1)} fusion(bf16[56,96]{1,0:T(8,128)(2,1)S(1)} %get-tuple-element.8, bf16[56,96]{1,0:T(8,128)(2,1)S(1)} %get-tuple-element.7), kind=kLoop, calls=%fused_computation.6 | loop fusion | flops 96768 | bytes 53760 | tf_op jit(solution)/shard_map/concatenate | solution.py:240
  4.3 0.7 %broadcast_in_dim.2.send_ref = s32[192,128]{1,0:T(8,128)} broadcast(s32[192]{0:T(256)S(1)} %pad_add_fusion), dimensions={0} | broadcast | bytes 99072 | tf_op jit(solution)/shard_map/broadcast_in_dim | solution.py:263
  5.0 0.0 copy-done.3
  5.1 0.0 copy-start.2
  5.1 0.9 %pad_maximum_fusion.1.w_ref = bf16[432,168]{1,0:T(8,128)(2,1)} fusion(bf16[432,56]{1,0:T(8,128)(2,1)S(1)} %get-tuple-element.6, bf16[432,56]{1,0:T(8,128)(2,1)S(1)} %get-tuple-element.5), kind=kLoop, calls=%fused_computation.5 | loop fusion | flops 435456 | bytes 241920 | tf_op jit(solution)/shard_map/concatenate | solution.py:240
  6.0 0.0 copy-done.2
  6.0 0.7 %copy.23.jac_ref = f32[3,9,9,128]{3,2,1,0:T(8,128)} copy(f32[3,9,9,128]{3,0,2,1:T(4,128)S(1)} %copy-done.2) | data formatting | bytes 248832 | tf_op args[1]
  6.7 0.3 copy-done
  7.0 0.7 %copy.24.fl_ref = f32[4,9,9,128]{3,2,1,0:T(8,128)} copy(f32[4,9,9,128]{3,0,2,1:T(4,128)S(1)} %copy-done) | data formatting | bytes 331776 | tf_op args[2]
  7.7 0.2 copy-done.1
  8.0 0.8 %copy.25.fn_ref = f32[4,9,9,128]{3,2,1,0:T(8,128)} copy(f32[4,9,9,128]{3,0,2,1:T(4,128)S(1)} %copy-done.1) | data formatting | bytes 331776 | tf_op args[3]
  8.7 50.2 %shard_map.127 = f32[9,56,128]{2,1,0:T(8,128)} custom-call(f32[9,56,128]{2,1,0:T(8,128)} %u_ref.1, f32[3,9,9,128]{3,2,1,0:T(8,128)} %copy.23.jac_ref, f32[4,9,9,128]{3,2,1,0:T(8,128)} %copy.24.fl_ref, f32[4,9,9,128]{3,2,1,0:T(8,128)} %copy.25.fn_ref, bf16[432,168]{1,0:T(8,128)(2,1)} %pad_maximum_fusion.1.w_ref, bf16[56,288]{1,0:T(8,128)(2,1)} %pad_maximum_fusion.2.lift_ref, ...), custom_call_target="tpu_custom_call" | custom-call | tf_op jit(solution)/shard_map/pallas_call | solution.py:268
  58.9 1.7 %copy.29 = f32[9,56,128]{2,1,0:T(8,128)} copy(f32[9,56,128]{2,1,0:T(8,128)} %shard_map.127) | data formatting | bytes 516096
  (12 shorter events, 0.1 us)
Async XLA Ops:
  0.0 0.7 %copy-start.8 = (s32[128]{0:T(128)S(1)}, s32[128]{0:T(128)}, u32[]{:S(2)}) copy-start(s32[128]{0:T(128)} %param.21) | copy-start | bytes 1540
  0.0 1.1 %copy-start.6 = (s32[1,4,16]{2,1,0:T(4,128)S(1)}, s32[1,4,16]{2,1,0:T(4,128)}, u32[]{:S(2)}) copy-start(s32[1,4,16]{2,1,0:T(4,128)} %param.24) | copy-start | bytes 772
  1.1 0.7 %copy-start.7 = (s32[1,128]{1,0:T(1,128)S(1)}, s32[1,128]{1,0:T(1,128)}, u32[]{:S(2)}) copy-start(s32[1,128]{1,0:T(1,128)} %param.25) | copy-start | bytes 1540
  2.7 0.8 %copy-start.5 = (f32[4,56,21]{1,0,2:T(4,128)S(1)}, f32[4,56,21]{1,0,2:T(4,128)}, u32[]{:S(2)}) copy-start(f32[4,56,21]{1,0,2:T(4,128)} %param.20) | copy-start | bytes 56452
  3.6 1.5 %copy-start.3 = (f32[3,56,56]{2,1,0:T(8,128)S(1)}, f32[3,56,56]{2,1,0:T(8,128)}, u32[]{:S(2)}) copy-start(f32[3,56,56]{2,1,0:T(8,128)} %param.18) | copy-start | bytes 112900
  3.6 1.4 %copy-start.4 = (f32[3,56,56]{2,1,0:T(8,128)S(1)}, f32[3,56,56]{2,1,0:T(8,128)}, u32[]{:S(2)}) copy-start(f32[3,56,56]{2,1,0:T(8,128)} %param.17) | copy-start | bytes 112900
  5.1 0.9 %copy-start.2 = (f32[3,9,9,128]{3,0,2,1:T(4,128)S(1)}, f32[3,9,9,128]{3,0,2,1:T(4,128)}, u32[]{:S(2)}) copy-start(f32[3,9,9,128]{3,0,2,1:T(4,128)} %param.14) | copy-start | bytes 373252
  6.0 1.0 %copy-start = (f32[4,9,9,128]{3,0,2,1:T(4,128)S(1)}, f32[4,9,9,128]{3,0,2,1:T(4,128)}, u32[]{:S(2)}) copy-start(f32[4,9,9,128]{3,0,2,1:T(4,128)} %param.15) | copy-start | bytes 497668
  7.0 1.0 %copy-start.1 = (f32[4,9,9,128]{3,0,2,1:T(4,128)S(1)}, f32[4,9,9,128]{3,0,2,1:T(4,128)}, u32[]{:S(2)}) copy-start(f32[4,9,9,128]{3,0,2,1:T(4,128)} %param.16) | copy-start | bytes 497668
where the time goes:
time: 60.9 us; the launch traced here: 60.5 us
  Pallas kernels  50.2 us (82%)
  local copies, waits for them, and re-layouts  8.1 us (13%)
  other arithmetic  2.22 us (4%)
    pallas_call x1, Pallas kernels, local(): pl.pallas_call(functools.partial(kernel, sizes), out_shape=jax.ShapeDtype...  50.2 us
    unnamed x24, local copies, waits for them, and re-layouts  7.22 us
    concatenate x2, other arithmetic, three_terms(): return jnp.concatenate([hi, hi, lo], axis=1).astype(BF16)  1.6 us

commit v1 on v0

--- a/solution.py
+++ b/solution.py
@@ -47,10 +47,30 @@
     return jnp.dot(a, b, preferred_element_type=F32)
 
 
+def three_terms(m):
+    n = m.shape[1]
+    hi, lo = split(m)
+    row = lax.broadcasted_iota(jnp.int32, (n, 3 * n), 0)
+    col = lax.broadcasted_iota(jnp.int32, (n, 3 * n), 1)
+    twice = jnp.where((col == row) | (col == row + n), 1.0, 0.0).astype(BF16)
+    last = jnp.where(col == row + 2 * n, 1.0, 0.0).astype(BF16)
+    return (dot(hi.astype(BF16), twice) + dot(lo.astype(BF16), last)).astype(BF16)
+
+
+def by_face(ref, width):
+    fb, _, b = ref.shape
+    rows = []
+    for j in range(4):
+        rows += [ref[:, j, :], jnp.zeros((width - fb, b), F32)]
+    return jnp.concatenate(rows, axis=0)
+
+
 def kernel(
     sizes,
-    u_ref, jac_ref, fl_ref, fn_ref, w_ref, lift_ref, len_ref, adj_ref, nf_ref, send_ref,
+    u_ref, jac_ref, fl_ref, fn_ref, stiff_ref, vol_ref, fp_ref, lb_ref,
+    cluster_ref, adj_ref, nf_ref, sub_ref, dom_ref,
     out_ref,
+    w_ref, lift_ref, send_ref,
     cur, piece, own, acc_g, proj, tproj, tr, oh, ohs, wl, jin, jrecv, outbuf, arr,
     ssem, rsem, jssem, jrsem,
 ):
@@ -107,6 +127,25 @@
         c.start()
     self_rows(jin, jrecv)
 
+    w_ref[...] = three_terms(jnp.concatenate([
+        stiff_ref[...].reshape(nd, B), vol_ref[...].reshape(nd, B),
+        by_face(fp_ref, FB)], axis=0))
+    back = by_face(lb_ref, FB)
+    back = jnp.concatenate([back, jnp.zeros((back.shape[0], 128 - B), F32)], axis=1)
+    back = jnp.concatenate([back, jnp.zeros((128 - back.shape[0], 128), F32)], axis=0)
+    lift_ref[...] = three_terms(back.T[:B, :ns])
+
+    def column(row):
+        n = row.shape[1]
+        eye = (lax.broadcasted_iota(jnp.int32, (n, n), 0)
+               == lax.broadcasted_iota(jnp.int32, (n, n), 1))
+        col = jnp.sum(jnp.where(eye, row.astype(F32), 0.0), axis=1, keepdims=True)
+        return jnp.broadcast_to(col, (n, E))
+
+    for p in range(n_sub):
+        send_ref[pl.ds(p * hs, hs), :] = column(sub_ref[pl.ds(p, 1), :])
+    send_ref[pl.ds(S, 2 * hd), :] = column(dom_ref[...])
+
     if RP > R:
         for t in range(TICKS):
             arr[t, pl.ds(R, RP - R), :] = jnp.zeros((RP - R, arr.shape[2]), F32)
@@ -121,7 +160,7 @@
                 for p in range(Q):
                     v = proj[pl.ds(d * B, B), pl.ds(p * E, E)]
                     for g in range(3):
-                        term = jac_ref[d, p, pl.ds(q0 + g, 1), :] * v
+                        term = jac_ref[p, q0 + g, pl.ds(d, 1), :] * v
                         sums[g] = term if sums[g] is None else sums[g] + term
             for g in range(3):
                 dst(q0 + g, sums[g])
@@ -130,14 +169,15 @@
         cur[q] = v
 
     weights = taylor_weights(ORDER)
-    length = len_ref[...]
+    group = cluster_ref[...]
+    length = jnp.where(group == 0, 1, jnp.where(group == 1, 2, 4))
 
     def flux(solver, i, trace):
         sums = [None] * Q
         for p in range(Q):
             v = trace(p)
             for q in range(Q):
-                term = solver[i, p, pl.ds(q, 1), :] * v
+                term = solver[p, q, pl.ds(i, 1), :] * v
                 sums[q] = term if sums[q] is None else sums[q] + term
         return sums
 
@@ -180,7 +220,7 @@
                 c.wait()
             want = jrecv[...]
             for j in range(4):
-                lane = lax.broadcasted_iota(jnp.int32, (R, E), 1)
+                lane = lax.broadcasted_iota(jnp.int32, (R, E), 1).astype(F32)
                 same = jnp.where(lane == send_ref[...], 1.0, 0.0)
                 face = jnp.where(want == F32(j), 1.0, 0.0)
                 ohs[:, pl.ds(j * E, E)] = (same * face).astype(BF16)
@@ -234,12 +274,6 @@
     lax.fori_loop(0, TICKS, tick, 0)
 
 
-def three_terms(m):
-    hi = lax.reduce_precision(m, 8, 7)
-    lo = lax.reduce_precision(m - hi, 8, 7)
-    return jnp.concatenate([hi, hi, lo], axis=1).astype(BF16)
-
-
 def local(
     n_dom, n_sub,
     unknowns, jacobians, flux_local, flux_neighbour, stiffness, volume_stiffness,
@@ -252,15 +286,6 @@
     hd = dom_sends.shape[1] // 2
     R = n_sub * hs + 2 * hd
     RP = round_up(R, 128)
-    pad = ((0, 0), (0, FB - fb), (0, 0))
-    w = three_terms(jnp.concatenate([
-        stiffness.reshape(3 * B, B), volume_stiffness.reshape(3 * B, B),
-        jnp.pad(face_proj, pad).reshape(4 * FB, B)], axis=0))
-    lift = three_terms(
-        jnp.pad(lift_back.transpose(1, 0, 2), pad[:1] + ((0, 0), (0, FB - fb))).reshape(B, 4 * FB))
-    length = jnp.left_shift(1, cluster).astype(jnp.int32).reshape(1, E)
-    sends = jnp.concatenate([sub_sends[0].reshape(-1), dom_sends[0]])
-    sends = jnp.broadcast_to(sends[:, None], (R, E))
     sizes = (Q, B, E, FB, n_dom, n_sub, hs, hd)
     peers = n_sub + 1
     vm = pl.BlockSpec(memory_space=pltpu.VMEM)
@@ -268,9 +293,12 @@
     return pl.pallas_call(
         functools.partial(kernel, sizes),
         out_shape=jax.ShapeDtypeStruct(unknowns.shape, F32),
-        in_specs=[vm] * 10,
+        in_specs=[vm] * 13,
         out_specs=vm,
         scratch_shapes=[
+            pltpu.VMEM((6 * B + 4 * FB, 3 * B), BF16),
+            pltpu.VMEM((B, 12 * FB), BF16),
+            pltpu.VMEM((R, E), F32),
             pltpu.VMEM((Q, B, E), F32),
             pltpu.VMEM((Q, B, E), F32),
             pltpu.VMEM((Q, B, E), F32),
@@ -291,8 +319,10 @@
             pltpu.SemaphoreType.DMA((peers,)),
         ],
         compiler_params=pltpu.CompilerParams(collective_id=0, has_side_effects=True),
-    )(unknowns, jacobians, flux_local, flux_neighbour, w, lift, length,
-      adjacent_column_index, neighbour_face, sends)
+    )(unknowns, jacobians.transpose(1, 2, 0, 3), flux_local.transpose(1, 2, 0, 3),
+      flux_neighbour.transpose(1, 2, 0, 3), stiffness, volume_stiffness,
+      face_proj.transpose(1, 0, 2), lift_back.transpose(2, 0, 1), cluster.reshape(1, E),
+      adjacent_column_index, neighbour_face, sub_sends[0], dom_sends)
 
 
 def solution(mesh):

time: 60.9 us -> 52.2 us (0.86)
  local copies, waits for them, and re-layouts: 8.1 us -> 1.66 us
  other arithmetic: 2.22 us -> 0 us
    unnamed x24 -> x1, local copies, waits for them, and re-layouts: 7.22 us -> 1.66 us
    concatenate x3 -> x0, other arithmetic: 1.68 us -> none  [the longest x2 1.6 us: three_terms(): return jnp.concatenate([hi, hi, lo], axis=1).astype(BF16)]
    broadcast_in_dim x1 -> x0, local copies, waits for them, and re-layouts: 0.72 us -> none  [local(): sends = jnp.broadcast_to(sends[:, None], (R, E))]
where the time goes in v1:
time: 52.2 us; the launch traced here: 52 us
  Pallas kernels  50.4 us (97%)
  local copies, waits for them, and re-layouts  1.66 us (3%)
    pallas_call x1, Pallas kernels, local(): pl.pallas_call(functools.partial(kernel, sizes), out_shape=jax.ShapeDtype...  50.4 us
    unnamed x1, local copies, waits for them, and re-layouts  1.66 us

profile of v1, /device:TPU:0, one launch (start us, length us, event | category | flops | bytes accessed | tf_op | source)
XLA Modules:
  0.0 52.0 jit_solution(16419276950271295370)
XLA Ops:
  0.0 50.4 %shard_map.127 = f32[9,56,128]{2,1,0:T(8,128)} custom-call(f32[9,56,128]{2,1,0:T(8,128)} %u_ref.1, f32[9,9,3,128]{3,2,1,0:T(4,128)} %bitcast.7, f32[9,9,4,128]{3,2,1,0:T(4,128)} %bitcast.8, f32[9,9,4,128]{3,2,1,0:T(4,128)} %bitcast.9, f32[3,56,56]{2,1,0:T(8,128)} %stiff_ref.1, f32[3,56,56]{2,1,0:T(8,128)} %vol_ref.1, f32[21,4,56]{2,1,0:T(4,128)} %bitcast.10, ...), custom_call_target="tpu_custom_call" | custom-call | tf_op jit(solution)/shard_map/pallas_call | solution.py:293
  50.4 1.7 %copy.15 = f32[9,56,128]{2,1,0:T(8,128)} copy(f32[9,56,128]{2,1,0:T(8,128)} %shard_map.127) | data formatting | bytes 516096

commit v2 on v1

--- a/solution.py
+++ b/solution.py
@@ -71,7 +71,7 @@
     cluster_ref, adj_ref, nf_ref, sub_ref, dom_ref,
     out_ref,
     w_ref, lift_ref, send_ref,
-    cur, piece, own, acc_g, proj, tproj, tr, oh, ohs, wl, jin, jrecv, outbuf, arr,
+    cur, piece, own, deriv, tacc, proj, tproj, tr, jac2, jac4, fl2, fl4, fn2, fn4, oh, ohs, jin, jrecv, outbuf, arr,
     ssem, rsem, jssem, jrsem,
 ):
     Q, B, E, FB, n_dom, n_sub, hs, hd = sizes
@@ -150,62 +150,108 @@
         for t in range(TICKS):
             arr[t, pl.ds(R, RP - R), :] = jnp.zeros((RP - R, arr.shape[2]), F32)
     out_ref[...] = u_ref[...]
-    own[...] = jnp.zeros_like(own)
-    acc_g[...] = jnp.zeros_like(acc_g)
-
-    def contract(dst):
+    lane = lax.broadcasted_iota(jnp.int32, (1, E), 1)
+
+    def tiles_of(G):
+        return -(-Q // G)
+
+    def select(blocks, G):
+        w = E // G
+        x = blocks[0]
+        for g in range(1, G):
+            other = blocks[g] if g < len(blocks) else jnp.zeros_like(x)
+            x = jnp.where((lane >= g * w) & (lane < (g + 1) * w), other, x)
+        return x
+
+    def pack(get, G):
+        made = []
+        for n in range(tiles_of(G)):
+            blocks = []
+            for g in range(min(G, Q - G * n)):
+                v = get(G * n + g)
+                blocks.append(pltpu.roll(v, g * (E // G), 1) if g else v)
+            made.append(select(blocks, G))
+        return made
+
+    def reduce_groups(v, G):
+        while G > 1:
+            G //= 2
+            v = v + pltpu.roll(v, E // 2 if G == 1 else E // (2 * G), 1)
+        return v
+
+    for src, halves, quarters in ((jac_ref, jac2, jac4), (fl_ref, fl2, fl4), (fn_ref, fn2, fn4)):
+        for G, dst in ((2, halves), (4, quarters)):
+            for q in range(Q):
+                for n, v in enumerate(pack(lambda p: src[p, q], G)):
+                    dst[n, q] = v
+    jacs = {1: jac_ref, 2: jac2, 4: jac4}
+    locals_ = {1: fl_ref, 2: fl2, 4: fl4}
+    neighbours = {1: fn_ref, 2: fn2, 4: fn4}
+
+    def contract(dst, G):
+        jac = jacs[G]
         for q0 in range(0, Q, 3):
             sums = [None] * 3
             for d in range(3):
-                for p in range(Q):
-                    v = proj[pl.ds(d * B, B), pl.ds(p * E, E)]
+                for n in range(tiles_of(G)):
+                    v = proj[pl.ds(d * B, B), pl.ds(n * E, E)]
                     for g in range(3):
-                        term = jac_ref[p, q0 + g, pl.ds(d, 1), :] * v
+                        term = jac[n, q0 + g, pl.ds(d, 1), :] * v
                         sums[g] = term if sums[g] is None else sums[g] + term
             for g in range(3):
-                dst(q0 + g, sums[g])
-
-    def put_cur(q, v):
-        cur[q] = v
+                dst(q0 + g, reduce_groups(sums[g], G))
 
     weights = taylor_weights(ORDER)
     group = cluster_ref[...]
     length = jnp.where(group == 0, 1, jnp.where(group == 1, 2, 4))
 
-    def flux(solver, i, trace):
-        sums = [None] * Q
-        for p in range(Q):
-            v = trace(p)
-            for q in range(Q):
-                term = solver[p, q, pl.ds(i, 1), :] * v
-                sums[q] = term if sums[q] is None else sums[q] + term
-        return sums
-
-    def tick(t, carry):
+    def predict(G):
+        T = tiles_of(G)
+        w = E // G
+        for n, v in enumerate(pack(lambda p: out_ref[p], G)):
+            cur[n] = v
+
+        def order_step(k, c):
+            proj[:, pl.ds(0, T * E)] = dot(
+                w_ref[pl.ds(0, nd), :], stacked_rhs([cur[n] for n in range(T)]))
+
+            def put(q, v):
+                n, g = q // G, q % G
+                if G == 1:
+                    cur[q] = v
+                    deriv[k, q] = v
+                    return
+                if g == 0:
+                    whole = Q - G * n >= G
+                    cur[n] = v if whole else jnp.where(lane < w, v, 0.0)
+                else:
+                    cur[n] = jnp.where((lane >= g * w) & (lane < (g + 1) * w), v, cur[n])
+                deriv[k, q] = jnp.where(lane < w, v, deriv[k, q])
+
+            contract(put, G)
+            return c
+
+        lax.fori_loop(1, ORDER, order_step, 0)
+
+    def tick(t):
+        G_in = {0: 1, 1: 4, 2: 2, 3: 4}[t]
+        G = {0: 4, 1: 2, 2: 4, 3: 1}[t]
+        T = tiles_of(G)
+        w = E // G
+        predict(G_in)
         phase = t & (length - 1)
+        rows = []
         for k in range(ORDER):
             row = jnp.full((1, E), weights[0][k], F32)
             for a in range(1, TICKS):
                 row = jnp.where(phase == a, F32(weights[a][k]), row)
-            wl[pl.ds(k, 1), :] = row
-        w0 = wl[pl.ds(0, 1), :]
+            rows.append(row)
         for p in range(Q):
-            v = out_ref[p]
-            cur[p] = v
-            piece[p] = w0 * v
-
-        def order_step(k, c):
-            proj[...] = dot(w_ref[pl.ds(0, nd), :], stacked_rhs([cur[p] for p in range(Q)]))
-            wk = wl[pl.ds(k, 1), :]
-
-            def put(q, v):
-                cur[q] = v
-                piece[q] = piece[q] + wk * v
-
-            contract(put)
-            return c
-
-        lax.fori_loop(1, ORDER, order_step, 0)
+            v = rows[0] * out_ref[p]
+            for k in range(1, ORDER):
+                v = v + rows[k] * deriv[k, p]
+            piece[p] = v
+            own[p] = v if t == 0 else own[p] + v
 
         tproj[...] = dot(
             w_ref[pl.ds(2 * nd, ns), :], stacked_rhs([piece[p] for p in range(Q)]))
@@ -214,14 +260,13 @@
                 tr[pl.ds(p * FB, FB), pl.ds(j * E, E)] = tproj[
                     pl.ds(j * FB, FB), pl.ds(p * E, E)]
 
-        @pl.when(t == 0)
-        def _():
+        if t == 0:
             for c in first:
                 c.wait()
             want = jrecv[...]
             for j in range(4):
-                lane = lax.broadcasted_iota(jnp.int32, (R, E), 1).astype(F32)
-                same = jnp.where(lane == send_ref[...], 1.0, 0.0)
+                spot = lax.broadcasted_iota(jnp.int32, (R, E), 1).astype(F32)
+                same = jnp.where(spot == send_ref[...], 1.0, 0.0)
                 face = jnp.where(want == F32(j), 1.0, 0.0)
                 ohs[:, pl.ds(j * E, E)] = (same * face).astype(BF16)
 
@@ -236,12 +281,14 @@
             c.start()
         self_rows(outbuf.at[t], arr.at[t])
 
-        for p in range(Q):
-            own[p] = own[p] + piece[p]
-        rhs = stacked_rhs([own[p] for p in range(Q)])
-        proj[...] = dot(w_ref[pl.ds(nd, nd), :], rhs)
-        tproj[...] = dot(w_ref[pl.ds(2 * nd, ns), :], rhs)
-        contract(put_cur)
+        rhs = stacked_rhs(pack(lambda p: own[p], G))
+        proj[:, pl.ds(0, T * E)] = dot(w_ref[pl.ds(nd, nd), :], rhs)
+        tproj[:, pl.ds(0, T * E)] = dot(w_ref[pl.ds(2 * nd, ns), :], rhs)
+
+        def put_cur(q, v):
+            cur[q] = v
+
+        contract(put_cur, G)
         ohl = oh[pl.ds(0, 4 * E), :]
         gathered = dot(hi, ohl) + dot(lo, ohl)
 
@@ -251,27 +298,42 @@
         ahi, alo = split(at)
         oha = oh[pl.ds(4 * E, RP), :]
         gathered = gathered + dot(ahi.astype(BF16), oha) + dot(alo.astype(BF16), oha)
-        tr[...] = gathered
-
-        finished = ((t + 1) & (length - 1)) == 0
+        tacc[...] = gathered if t == 0 else tacc[...] + gathered
+
         for i in range(4):
             rows = pl.ds(i * FB, FB)
-            there = flux(fn_ref, i, lambda p: tr[pl.ds(p * FB, FB), pl.ds(i * E, E)])
-            for q in range(Q):
-                acc_g[q, rows, :] = acc_g[q, rows, :] + there[q]
-            here = flux(fl_ref, i, lambda p: tproj[rows, pl.ds(p * E, E)])
-            for q in range(Q):
-                proj[rows, pl.ds(q * E, E)] = acc_g[q, rows, :] + here[q]
+            there = pack(lambda p: tacc[pl.ds(p * FB, FB), pl.ds(i * E, E)], G)
+            sums = [None] * Q
+            for n in range(T):
+                here = tproj[rows, pl.ds(n * E, E)]
+                for q in range(Q):
+                    term = (locals_[G][n, q, pl.ds(i, 1), :] * here
+                            + neighbours[G][n, q, pl.ds(i, 1), :] * there[n])
+                    sums[q] = term if sums[q] is None else sums[q] + term
+            sums = [reduce_groups(v, G) for v in sums]
+            for n in range(T):
+                proj[rows, pl.ds(n * E, E)] = select(sums[n * G:(n + 1) * G], G)
         lifted = dot(
-            lift_ref[...], stacked_rhs([proj[pl.ds(0, ns), pl.ds(q * E, E)] for q in range(Q)]))
+            lift_ref[...], stacked_rhs([proj[pl.ds(0, ns), pl.ds(n * E, E)] for n in range(T)]))
+        finished = ((t + 1) & (length - 1)) == 0
         for q in range(Q):
-            change = cur[q] - lifted[:, q * E:(q + 1) * E]
-            out_ref[q] = jnp.where(finished, out_ref[q] + change, out_ref[q])
-            own[q] = jnp.where(finished, 0.0, own[q])
-            acc_g[q] = jnp.where(finished, 0.0, acc_g[q])
-        return carry
-
-    lax.fori_loop(0, TICKS, tick, 0)
+            n, g = q // G, q % G
+            part = lifted[:, n * E:(n + 1) * E]
+            if g:
+                part = pltpu.roll(part, E - g * w, 1)
+            change = cur[q] - part
+            if t == TICKS - 1:
+                out_ref[q] = out_ref[q] + change
+            else:
+                out_ref[q] = jnp.where(finished, out_ref[q] + change, out_ref[q])
+                own[q] = jnp.where(finished, 0.0, own[q])
+        if t < TICKS - 1:
+            for i in range(4):
+                block = pl.ds(i * E, E)
+                tacc[:, block] = jnp.where(finished, 0.0, tacc[:, block])
+
+    for t in range(TICKS):
+        tick(t)
 
 
 def local(
@@ -302,13 +364,19 @@
             pltpu.VMEM((Q, B, E), F32),
             pltpu.VMEM((Q, B, E), F32),
             pltpu.VMEM((Q, B, E), F32),
-            pltpu.VMEM((Q, 4 * FB, E), F32),
+            pltpu.VMEM((ORDER, Q, B, E), F32),
+            pltpu.VMEM((W, 4 * E), F32),
             pltpu.VMEM((3 * B, Q * E), F32),
             pltpu.VMEM((4 * FB, Q * E), F32),
             pltpu.VMEM((W, 4 * E), F32),
+            pltpu.VMEM((-(-Q // 2), Q, 3, E), F32),
+            pltpu.VMEM((-(-Q // 4), Q, 3, E), F32),
+            pltpu.VMEM((-(-Q // 2), Q, 4, E), F32),
+            pltpu.VMEM((-(-Q // 4), Q, 4, E), F32),
+            pltpu.VMEM((-(-Q // 2), Q, 4, E), F32),
+            pltpu.VMEM((-(-Q // 4), Q, 4, E), F32),
             pltpu.VMEM((4 * E + RP, 4 * E), BF16),
             pltpu.VMEM((R, 4 * E), BF16),
-            pltpu.VMEM((8, E), F32),
             pltpu.VMEM((R, 128), F32),
             pltpu.VMEM((R, 128), F32),
             pltpu.VMEM((TICKS, R, W), F32),

time: 52.2 us -> 48 us (0.920)
  Pallas kernels: 50.4 us -> 46.2 us
    pallas_call x1, Pallas kernels: 50.4 us -> 46.2 us  [local(): pl.pallas_call(functools.partial(kernel, sizes), out_shape=jax.ShapeDtype...]
where the time goes in v2:
time: 48 us; the launch traced here: 47.8 us
  Pallas kernels  46.2 us (96%)
  local copies, waits for them, and re-layouts  1.66 us (3%)
    pallas_call x1, Pallas kernels, local(): pl.pallas_call(functools.partial(kernel, sizes), out_shape=jax.ShapeDtype...  46.2 us
    unnamed x1, local copies, waits for them, and re-layouts  1.66 us

profile of v2, /device:TPU:0, one launch (start us, length us, event | category | flops | bytes accessed | tf_op | source)
XLA Modules:
  0.0 47.8 jit_solution(12963165999047953012)
XLA Ops:
  0.0 46.2 %shard_map.127 = f32[9,56,128]{2,1,0:T(8,128)} custom-call(f32[9,56,128]{2,1,0:T(8,128)} %u_ref.1, f32[9,9,3,128]{3,2,1,0:T(4,128)} %bitcast.7, f32[9,9,4,128]{3,2,1,0:T(4,128)} %bitcast.8, f32[9,9,4,128]{3,2,1,0:T(4,128)} %bitcast.9, f32[3,56,56]{2,1,0:T(8,128)} %stiff_ref.1, f32[3,56,56]{2,1,0:T(8,128)} %vol_ref.1, f32[21,4,56]{2,1,0:T(4,128)} %bitcast.10, ...), custom_call_target="tpu_custom_call" | custom-call | tf_op jit(solution)/shard_map/pallas_call | solution.py:355
  46.2 1.7 %copy.15 = f32[9,56,128]{2,1,0:T(8,128)} copy(f32[9,56,128]{2,1,0:T(8,128)} %shard_map.127) | data formatting | bytes 516096
